TPU v7x, 32 devices: a whole 2x2x4 slice. The times are simulated.
32 devices in a mesh: band: 4 (over x, core), grid: 8 (over z, y).
Axes of the slice: x: 2, y: 2, z: 4, core: 2. Of those that a mesh axis runs over, the one named last changes fastest.
Arguments:
- orbitals: float32 [4, 128, 128, 128], P('band', 'grid'), may hold values from -4 to 10, as said below
- pivots: int32 [4], replicated, may hold values from 0 to 2097151, as said below
- pattern: int32 [4, 4], replicated, may hold values from 0 to 1, as said below
Outputs:
- localized: float32 [4, 128, 128, 128], P('band', 'grid')
- exchange_term: float32 [4, 128, 128, 128], P('band', 'grid')
Inputs may be any that keep to these rules, and one draw needn't show every extreme that they name: Values of the orbitals on the grid; the matrix of their values at the pivots has a Cholesky factorization. `pivots`: distinct flat cell indices; the first and the last cell of the grid are always among them. `pattern`: every diagonal entry is 1; each row holds 1 to 4 ones, some row exactly 4; the matrix holds exactly 8 ones.
All inputs are finite; a program needn't handle non-finite values.
Results may differ from a plain program's by a relative error of at most 0.0003.
Values sent between devices are 32-bit elements; how exact they have to be, the bound alone decides.
A program may use at most 64 MiB of HBM per device.

v0:
```python
import jax
import jax.numpy as jnp
from jax import lax
from jax.sharding import PartitionSpec as P

MOST_PARTNERS = 4
precise = lax.Precision.HIGHEST


def tables(length):
    across = jnp.arange(length, dtype=jnp.int32)
    phases = across[:, None] * across[None, :] % length
    angles = phases.astype(jnp.float32) * (2.0 * jnp.pi / length)
    return (jnp.cos(angles), jnp.sin(angles))


def wrapped(indices, length):
    return jnp.where(indices < length // 2, indices, indices - length)


def coulomb(length, plane_start, plane_count):
    wave_first = wrapped(jnp.arange(length, dtype=jnp.int32), length).astype(jnp.float32)
    wave_second = wrapped(plane_start + jnp.arange(plane_count, dtype=jnp.int32), length).astype(
        jnp.float32
    )
    squared = (
        wave_first[:, None, None] ** 2
        + wave_second[None, :, None] ** 2
        + wave_first[None, None, :] ** 2
    )
    scaling = float(length) ** 1.5
    return jnp.where(squared > 0, 0.25 / (scaling * jnp.maximum(squared, 1.0)), 0.0)


def densities(first_bands, second_bands):
    return (first_bands[:, None] * second_bands[None, :]).reshape((-1,) + first_bands.shape[1:])


def applied(potential, first_bands, second_bands):
    shaped = potential.reshape(
        (first_bands.shape[0], second_bands.shape[0]) + first_bands.shape[1:]
    )
    return jnp.sum(shaped * second_bands[None], axis=1)


def filtered(real_in, imag_in, kernel, cos_table, sin_table):
    real_part = jnp.dot(real_in, cos_table, precision=precise) + jnp.dot(
        imag_in, sin_table, precision=precise
    )
    imag_part = jnp.dot(imag_in, cos_table, precision=precise) - jnp.dot(
        real_in, sin_table, precision=precise
    )
    real_part, imag_part = (
        jnp.einsum("pxyz,yk->pxkz", real_part, cos_table, precision=precise)
        + jnp.einsum("pxyz,yk->pxkz", imag_part, sin_table, precision=precise),
        jnp.einsum("pxyz,yk->pxkz", imag_part, cos_table, precision=precise)
        - jnp.einsum("pxyz,yk->pxkz", real_part, sin_table, precision=precise),
    )
    real_wide = lax.all_to_all(real_part, "grid", split_axis=2, concat_axis=1, tiled=True)
    imag_wide = lax.all_to_all(imag_part, "grid", split_axis=2, concat_axis=1, tiled=True)
    ahead_real = (
        jnp.einsum("pxyz,xk->pkyz", real_wide, cos_table, precision=precise)
        + jnp.einsum("pxyz,xk->pkyz", imag_wide, sin_table, precision=precise)
    ) * kernel
    ahead_imag = (
        jnp.einsum("pxyz,xk->pkyz", imag_wide, cos_table, precision=precise)
        - jnp.einsum("pxyz,xk->pkyz", real_wide, sin_table, precision=precise)
    ) * kernel
    back_real = jnp.einsum("pxyz,xk->pkyz", ahead_real, cos_table, precision=precise) - jnp.einsum(
        "pxyz,xk->pkyz", ahead_imag, sin_table, precision=precise
    )
    back_imag = jnp.einsum("pxyz,xk->pkyz", ahead_imag, cos_table, precision=precise) + jnp.einsum(
        "pxyz,xk->pkyz", ahead_real, sin_table, precision=precise
    )
    real_part = lax.all_to_all(back_real, "grid", split_axis=1, concat_axis=2, tiled=True)
    imag_part = lax.all_to_all(back_imag, "grid", split_axis=1, concat_axis=2, tiled=True)
    real_part, imag_part = (
        jnp.einsum("pxyz,yk->pxkz", real_part, cos_table, precision=precise)
        - jnp.einsum("pxyz,yk->pxkz", imag_part, sin_table, precision=precise),
        jnp.einsum("pxyz,yk->pxkz", imag_part, cos_table, precision=precise)
        + jnp.einsum("pxyz,yk->pxkz", real_part, sin_table, precision=precise),
    )
    out_real = jnp.dot(real_part, cos_table, precision=precise) - jnp.dot(
        imag_part, sin_table, precision=precise
    )
    out_imag = jnp.dot(imag_part, cos_table, precision=precise) + jnp.dot(
        real_part, sin_table, precision=precise
    )
    return (out_real, out_imag)


def twin_potential(first_one, second_one, first_two, second_two, kernel, cos_table, sin_table):
    potential_one, potential_two = filtered(
        densities(first_one, second_one),
        densities(first_two, second_two),
        kernel,
        cos_table,
        sin_table,
    )
    return (
        applied(potential_one, first_one, second_one),
        applied(potential_two, first_two, second_two),
    )


def collect(wanted, portion):
    positions = jnp.arange(portion.shape[0], dtype=jnp.int32)
    chooser = (wanted[:, None] == positions[None, :]).astype(jnp.float32)
    return jnp.einsum("qm,mxyz->qxyz", chooser, portion, precision=precise)


def local(orbitals, pivots, pattern):
    band_dev = orbitals.shape[0]
    slab_planes = orbitals.shape[1]
    length = orbitals.shape[3]
    block_total = pattern.shape[0]
    grid_index = lax.axis_index("grid")
    band_index = lax.axis_index("band")
    cell_count = slab_planes * length * length
    flat_local = orbitals.reshape(band_dev, cell_count)
    local_cell = pivots - grid_index * cell_count
    inside = (local_cell >= 0) & (local_cell < cell_count)
    sampled = jnp.take(flat_local, jnp.clip(local_cell, 0, cell_count - 1), axis=1)
    partial_pick = jnp.where(inside[None, :], sampled, 0.0)
    own_rows = lax.psum(partial_pick, "grid")
    picked = lax.all_gather(own_rows, "band", axis=0, tiled=True)
    gram_matrix = jnp.dot(picked.T, picked, precision=precise)
    factor = jnp.linalg.cholesky(gram_matrix)
    rotation = lax.linalg.triangular_solve(factor, picked.T, left_side=True, lower=True).T
    own_weights = lax.dynamic_slice_in_dim(rotation, band_index * band_dev, band_dev, 0)
    localized = lax.psum_scatter(
        jnp.einsum("bk,bxyz->kxyz", own_weights, orbitals, precision=precise),
        "band",
        scatter_dimension=0,
        tiled=True,
    )
    cos_table, sin_table = tables(length)
    plane_count = length // lax.axis_size("grid")
    kernel = coulomb(length, grid_index * plane_count, plane_count)
    columns = jnp.arange(block_total, dtype=jnp.int32)
    members = jnp.arange(band_dev, dtype=jnp.int32)
    own_row = lax.dynamic_index_in_dim(pattern, band_index, 0, keepdims=False)
    before = jnp.cumsum(own_row) - own_row
    slot_ids = jnp.arange(MOST_PARTNERS, dtype=jnp.int32)
    matches = (own_row[None, :] == 1) & (before[None, :] == slot_ids[:, None])
    partner = jnp.sum(jnp.where(matches, columns[None, :], 0), axis=1)
    present = jnp.any(matches, axis=1)
    wanted = jnp.where(
        present[:, None], partner[:, None] * band_dev + members[None, :], -1
    ).reshape(-1)
    partners = collect(wanted, lax.all_gather(localized, "band", axis=0, tiled=True))
    exchange_term = jnp.zeros_like(localized)
    for couple in range(MOST_PARTNERS // 2):
        first_rows = partners[2 * couple * band_dev : (2 * couple + 1) * band_dev]
        second_rows = partners[(2 * couple + 1) * band_dev : (2 * couple + 2) * band_dev]
        term_one, term_two = twin_potential(
            localized, first_rows, localized, second_rows, kernel, cos_table, sin_table
        )
        exchange_term = exchange_term + term_one + term_two
    return (localized, exchange_term)


def solution(mesh):
    return jax.shard_map(
        local,
        mesh=mesh,
        in_specs=(P("band", "grid", None, None), P(), P()),
        out_specs=(P("band", "grid", None, None), P("band", "grid", None, None)),
        check_vma=False,
    )
```

profile of v0, /device:TPU:0, one launch (start us, length us, event | category | flops | bytes accessed | tf_op | source)
XLA Modules:
  0.0 410.0 jit_solution(14240325148722384985)
XLA Ops:
  10.0 23.1 %psum.7 = f32[1,4]{1,0:T(1,128)S(1)} all-reduce(f32[1,4]{1,0:T(1,128)S(1)} %fusion.210), channel_id=1, replica_groups=mesh['band'=4,'grid'=8] {'grid'}, use_global_device_ids=true, to_apply=%region_0.1 | all-reduce | flops 4 | bytes 32 | tf_op jit(solution)/shard_map/psum | solution.py:125
  33.1 5.0 %all-gather = f32[4,1,4]{2,1,0:T(1,128)S(1)} all-gather(f32[1,1,4]{2,1,0:T(1,128)S(1)} %bitcast.338), channel_id=1, replica_groups=mesh['band'=4,'grid'=8] {'band'}, dimensions={0}, use_global_device_ids=true | all-gather | bytes 80 | tf_op jit(solution)/shard_map/all_gather | solution.py:126
  40.6 3.8 broadcast_multiply_fusion
  44.4 41.9 %reduce-scatter.2.cloned.1.call-done = f32[1,16,128,128]{3,2,1,0:T(8,128)} async-done(((f32[4,16,128,128]{3,2,1,0:T(8,128)}), f32[1,16,128,128]{3,2,1,0:T(8,128)}) %reduce-scatter.2.cloned.1.call-update) | async-done | bytes 1048592 | tf_op jit(solution)/shard_map/reduce_scatter | solution.py:131
  87.5 35.6 %all-gather.3.cloned.1.call-done = f32[4,16,128,128]{3,2,1,0:T(8,128)} async-done(((f32[1,16,128,128]{3,2,1,0:T(8,128)}), f32[4,16,128,128]{3,2,1,0:T(8,128)}) %all-gather.3.cloned.1.call-update) | async-done | bytes 4194320 | tf_op jit(solution)/shard_map/all_gather | solution.py:151
  123.0 8.5 %fusion = f32[4,16,128,128]{3,0,2,1:T(4,128)S(1)} fusion(f32[4,16,128,128]{3,2,1,0:T(8,128)} %all-gather.3.cloned.1.call-done, s32[4]{0:T(128)S(1)} %broadcast_select_fusion), kind=kOutput, calls=%fused_computation.1 | convolution fusion | flops 50331664 | bytes 8388624 | tf_op jit(solution)/shard_map/qm,mxyz->qxyz/dot_general | solution.py:109
  131.6 3.6 slice_multiply_fusion.3
  145.2 5.8 %all-to-all-start.4 = ((f32[1,16,128,128]{3,1,0,2:T(8,128)}), f32[1,16,128,128]{3,1,0,2:T(8,128)}, u32[]{:S(2)}, u32[]{:S(2)}) async-start(f32[1,16,128,128]{3,1,0,2:T(8,128)} %copy.182), calls=%async_computation.5 | async-start | bytes 2097152 | tf_op jit(solution)/shard_map/all_to_all | solution.py:59
  152.3 2.5 fusion.8
  154.8 1.6 copy.187
  156.4 20.8 %all-to-all-done.4 = f32[1,16,128,128]{3,1,0,2:T(8,128)} async-done(((f32[1,16,128,128]{3,1,0,2:T(8,128)}), f32[1,16,128,128]{3,1,0,2:T(8,128)}, u32[]{:S(2)}, u32[]{:S(2)}) %all-to-all-start.4) | async-done | bytes 1048608 | tf_op jit(solution)/shard_map/all_to_all | solution.py:59
  177.2 4.2 %all-to-all-start.5 = ((f32[1,16,128,128]{3,1,0,2:T(8,128)}), f32[1,16,128,128]{3,1,0,2:T(8,128)}, u32[]{:S(2)}, u32[]{:S(2)}) async-start(f32[1,16,128,128]{3,1,0,2:T(8,128)} %copy.187), calls=%async_computation.6 | async-start | bytes 2097152 | tf_op jit(solution)/shard_map/all_to_all | solution.py:60
  190.5 16.5 %all-to-all-done.5 = f32[1,16,128,128]{3,1,0,2:T(8,128)} async-done(((f32[1,16,128,128]{3,1,0,2:T(8,128)}), f32[1,16,128,128]{3,1,0,2:T(8,128)}, u32[]{:S(2)}, u32[]{:S(2)}) %all-to-all-start.5) | async-done | bytes 1048608 | tf_op jit(solution)/shard_map/all_to_all | solution.py:60
  207.1 4.0 all-to-all-start.1
  213.7 1.6 copy.156
  215.3 21.6 %all-to-all-done.1 = f32[1,16,128,128]{3,1,0,2:T(8,128)S(1)} async-done(((f32[1,16,128,128]{3,1,0,2:T(8,128)}), f32[1,16,128,128]{3,1,0,2:T(8,128)S(1)}, u32[]{:S(2)}, u32[]{:S(2)}) %all-to-all-start.1) | async-done | bytes 1048608 | tf_op jit(solution)/shard_map/all_to_all | solution.py:60
  236.8 3.6 all-to-all-start
  251.4 1.6 copy.194
  253.0 13.5 %all-to-all-done = f32[1,16,128,128]{3,1,0,2:T(8,128)S(1)} async-done(((f32[1,16,128,128]{3,1,0,2:T(8,128)}), f32[1,16,128,128]{3,1,0,2:T(8,128)S(1)}, u32[]{:S(2)}, u32[]{:S(2)}) %all-to-all-start) | async-done | bytes 1048608 | tf_op jit(solution)/shard_map/all_to_all | solution.py:59
  267.4 3.8 all-to-all-start.6
  273.8 1.6 copy.199
  275.4 21.8 %all-to-all-done.6 = f32[1,128,16,128]{3,2,0,1:T(8,128)S(1)} async-done(((f32[1,128,16,128]{3,2,0,1:T(8,128)}), f32[1,128,16,128]{3,2,0,1:T(8,128)S(1)}, u32[]{:S(2)}, u32[]{:S(2)}) %all-to-all-start.6) | async-done | bytes 1048608 | tf_op jit(solution)/shard_map/all_to_all | solution.py:75
  297.2 4.2 %all-to-all-start.7 = ((f32[1,128,16,128]{3,2,0,1:T(8,128)}), f32[1,128,16,128]{3,2,0,1:T(8,128)}, u32[]{:S(2)}, u32[]{:S(2)}) async-start(f32[1,128,16,128]{3,2,0,1:T(8,128)} %copy.199), calls=%async_computation.8 | async-start | bytes 2097152 | tf_op jit(solution)/shard_map/all_to_all | solution.py:76
  309.8 1.6 copy.173
  311.4 15.6 %all-to-all-done.7 = f32[1,128,16,128]{3,2,0,1:T(8,128)} async-done(((f32[1,128,16,128]{3,2,0,1:T(8,128)}), f32[1,128,16,128]{3,2,0,1:T(8,128)}, u32[]{:S(2)}, u32[]{:S(2)}) %all-to-all-start.7) | async-done | bytes 1048608 | tf_op jit(solution)/shard_map/all_to_all | solution.py:76
  327.1 4.6 %all-to-all-start.3 = ((f32[1,128,16,128]{3,2,0,1:T(8,128)}), f32[1,128,16,128]{3,2,0,1:T(8,128)}, u32[]{:S(2)}, u32[]{:S(2)}) async-start(f32[1,128,16,128]{3,2,0,1:T(8,128)} %copy.173), calls=%async_computation.4 | async-start | bytes 2097152 | tf_op jit(solution)/shard_map/all_to_all | solution.py:76
  334.3 1.6 copy.168
  337.3 2.3 fusion.48
  339.6 17.5 %all-to-all-done.3 = f32[1,128,16,128]{3,2,0,1:T(8,128)} async-done(((f32[1,128,16,128]{3,2,0,1:T(8,128)}), f32[1,128,16,128]{3,2,0,1:T(8,128)}, u32[]{:S(2)}, u32[]{:S(2)}) %all-to-all-start.3) | async-done | bytes 1048608 | tf_op jit(solution)/shard_map/all_to_all | solution.py:76
  357.1 4.2 %all-to-all-start.2 = ((f32[1,128,16,128]{3,2,0,1:T(8,128)}), f32[1,128,16,128]{3,2,0,1:T(8,128)}, u32[]{:S(2)}, u32[]{:S(2)}) async-start(f32[1,128,16,128]{3,2,0,1:T(8,128)} %copy.168), calls=%async_computation.3 | async-start | bytes 2097152 | tf_op jit(solution)/shard_map/all_to_all | solution.py:75
  371.6 15.2 %all-to-all-done.2 = f32[1,128,16,128]{3,2,0,1:T(8,128)} async-done(((f32[1,128,16,128]{3,2,0,1:T(8,128)}), f32[1,128,16,128]{3,2,0,1:T(8,128)}, u32[]{:S(2)}, u32[]{:S(2)}) %all-to-all-start.2) | async-done | bytes 1048608 | tf_op jit(solution)/shard_map/all_to_all | solution.py:75
  398.4 4.5 %multiply_add_fusion = f32[1,16,128,128]{3,0,2,1:T(1,128)} fusion(f32[1,16,128,128]{3,0,2,1:T(1,128)S(1)} %bitcast.318, f32[1,16,128,128]{3,0,2,1:T(1,128)S(1)} %bitcast.317, f32[1,16,128,128]{3,0,2,1:T(1,128)S(1)} %bitcast.319, f32[1,16,128,128]{3,0,2,1:T(1,128)S(1)} %bitcast.320, f32[4,16,128,128]{3,0,2,1:T(4,128)S(1)} %copy-done.1), kind=kLoop, calls=%fused_computation.49 | loop fusion | flops 1835008 | bytes 9437184 | tf_op jit(solution)/shard_map/add | solution.py:159
  (101 shorter events, 77.8 us)
Async XLA Ops:
  7.2 79.1 %reduce-scatter.2.cloned.1.call-start = ((), (), s32[]{:S(2)}) async-start(), calls=%async_computation.9 | async-start | bytes 5242880 | tf_op jit(solution)/shard_map/reduce_scatter | solution.py:131
  44.4 78.6 %all-gather.3.cloned.1.call-start = ((), (), s32[]{:S(2)}) async-start(), calls=%async_computation.10 | async-start | bytes 5242880 | tf_op jit(solution)/shard_map/all_gather | solution.py:151
  87.5 44.1 %copy-start.3 = (f32[1,16,128,128]{3,2,1,0:T(8,128)S(1)}, f32[1,16,128,128]{3,2,1,0:T(8,128)}, u32[]{:S(2)}) copy-start(f32[1,16,128,128]{3,2,1,0:T(8,128)} %reduce-scatter.2.cloned.1.call-done) | copy-start | bytes 3145732
  131.6 3.6 copy-start
  140.1 1.0 copy-start.2
  145.2 32.0 %all-to-all-start.4 = ((f32[1,16,128,128]{3,1,0,2:T(8,128)}), f32[1,16,128,128]{3,1,0,2:T(8,128)}, u32[]{:S(2)}, u32[]{:S(2)}) async-start(f32[1,16,128,128]{3,1,0,2:T(8,128)} %copy.182), calls=%async_computation.5 | async-start | bytes 2097152 | tf_op jit(solution)/shard_map/all_to_all | solution.py:59
  177.2 29.9 %all-to-all-start.5 = ((f32[1,16,128,128]{3,1,0,2:T(8,128)}), f32[1,16,128,128]{3,1,0,2:T(8,128)}, u32[]{:S(2)}, u32[]{:S(2)}) async-start(f32[1,16,128,128]{3,1,0,2:T(8,128)} %copy.187), calls=%async_computation.6 | async-start | bytes 2097152 | tf_op jit(solution)/shard_map/all_to_all | solution.py:60
  207.1 29.7 %all-to-all-start.1 = ((f32[1,16,128,128]{3,1,0,2:T(8,128)}), f32[1,16,128,128]{3,1,0,2:T(8,128)S(1)}, u32[]{:S(2)}, u32[]{:S(2)}) async-start(f32[1,16,128,128]{3,1,0,2:T(8,128)} %copy.161), calls=%async_computation.2 | async-start | bytes 2097152 | tf_op jit(solution)/shard_map/all_to_all | solution.py:60
  236.8 7.7 %copy-start.5 = (f32[1,16,128,128]{3,1,0,2:T(8,128)}, f32[1,16,128,128]{3,1,0,2:T(8,128)S(1)}, u32[]{:S(2)}) copy-start(f32[1,16,128,128]{3,1,0,2:T(8,128)S(1)} %all-to-all-done.1) | copy-start | bytes 3145732
  236.8 29.6 %all-to-all-start = ((f32[1,16,128,128]{3,1,0,2:T(8,128)}), f32[1,16,128,128]{3,1,0,2:T(8,128)S(1)}, u32[]{:S(2)}, u32[]{:S(2)}) async-start(f32[1,16,128,128]{3,1,0,2:T(8,128)} %copy.156), calls=%async_computation.1 | async-start | bytes 2097152 | tf_op jit(solution)/shard_map/all_to_all | solution.py:59
  266.4 1.0 copy-start.7
  267.4 29.8 %all-to-all-start.6 = ((f32[1,128,16,128]{3,2,0,1:T(8,128)}), f32[1,128,16,128]{3,2,0,1:T(8,128)S(1)}, u32[]{:S(2)}, u32[]{:S(2)}) async-start(f32[1,128,16,128]{3,2,0,1:T(8,128)} %copy.194), calls=%async_computation.7 | async-start | bytes 2097152 | tf_op jit(solution)/shard_map/all_to_all | solution.py:75
  272.5 28.9 %copy-start.6 = (f32[1,16,128,128]{3,1,0,2:T(8,128)S(1)}, f32[1,16,128,128]{3,1,0,2:T(8,128)}, u32[]{:S(2)}) copy-start(f32[1,16,128,128]{3,1,0,2:T(8,128)} %copy-done.5) | copy-start | bytes 3145732
  273.8 27.7 %copy-start.8 = (f32[1,16,128,128]{3,1,0,2:T(8,128)S(1)}, f32[1,16,128,128]{3,1,0,2:T(8,128)}, u32[]{:S(2)}) copy-start(f32[1,16,128,128]{3,1,0,2:T(8,128)} %copy-done.7) | copy-start | bytes 3145732
  297.2 29.9 %all-to-all-start.7 = ((f32[1,128,16,128]{3,2,0,1:T(8,128)}), f32[1,128,16,128]{3,2,0,1:T(8,128)}, u32[]{:S(2)}, u32[]{:S(2)}) async-start(f32[1,128,16,128]{3,2,0,1:T(8,128)} %copy.199), calls=%async_computation.8 | async-start | bytes 2097152 | tf_op jit(solution)/shard_map/all_to_all | solution.py:76
  327.1 30.1 %all-to-all-start.3 = ((f32[1,128,16,128]{3,2,0,1:T(8,128)}), f32[1,128,16,128]{3,2,0,1:T(8,128)}, u32[]{:S(2)}, u32[]{:S(2)}) async-start(f32[1,128,16,128]{3,2,0,1:T(8,128)} %copy.173), calls=%async_computation.4 | async-start | bytes 2097152 | tf_op jit(solution)/shard_map/all_to_all | solution.py:76
  357.1 29.7 %all-to-all-start.2 = ((f32[1,128,16,128]{3,2,0,1:T(8,128)}), f32[1,128,16,128]{3,2,0,1:T(8,128)}, u32[]{:S(2)}, u32[]{:S(2)}) async-start(f32[1,128,16,128]{3,2,0,1:T(8,128)} %copy.168), calls=%async_computation.3 | async-start | bytes 2097152 | tf_op jit(solution)/shard_map/all_to_all | solution.py:75
  362.7 4.0 copy-start.4
  394.7 3.7 copy-start.1
Sparse Core Ops, SparseCore 0:
  44.5 41.7 reduce-scatter.1
  88.5 34.4 all-gather.2
where the time goes:
time: 417 us; the launch traced here: 410 us
  waiting for transfers between devices  220 us (53%)
  matrix products  72.7 us (17%)
  starting transfers between devices  34.7 us (8%)
  blocking collectives  28.1 us (7%)
  local copies, waits for them, and re-layouts  23.3 us (6%)
  other arithmetic  16.4 us (4%)
  between operations  14.9 us (4%)
    reduce_scatter x1, waiting for transfers between devices, local(): lax.psum_scatter(jnp.einsum('bk,bxyz->kxyz', own_weights, orbitals, preci...  41.9 us
    all_to_all x2, waiting for transfers between devices, filtered(): lax.all_to_all(imag_part, 'grid', split_axis=2, concat_axis=1, tiled=True)  38.1 us
    all_to_all x2, waiting for transfers between devices, filtered(): lax.all_to_all(back_real, 'grid', split_axis=1, concat_axis=2, tiled=True)  36.9 us
    all_gather x1, waiting for transfers between devices, local(): lax.all_gather(localized, 'band', axis=0, tiled=True)  35.6 us
    all_to_all x2, waiting for transfers between devices, filtered(): lax.all_to_all(real_part, 'grid', split_axis=2, concat_axis=1, tiled=True)  34.3 us
    all_to_all x2, waiting for transfers between devices, filtered(): lax.all_to_all(back_imag, 'grid', split_axis=1, concat_axis=2, tiled=True)  33.2 us
    psum x1, blocking collectives, local(): own_rows = lax.psum(partial_pick, 'grid')  23.1 us
    all_to_all x2, starting transfers between devices, filtered(): lax.all_to_all(real_part, 'grid', split_axis=2, concat_axis=1, tiled=True)  9.43 us
  transfers between devices with their start and end apart: 10, of which 10 were waited for; matrix products, arithmetic and copies ran while one was open for 16% of the time, Pallas kernels for 0%

commit v1 on v0

--- a/solution.py
+++ b/solution.py
@@ -56,7 +56,12 @@
         jnp.einsum("pxyz,yk->pxkz", imag_part, cos_table, precision=precise)
         - jnp.einsum("pxyz,yk->pxkz", real_part, sin_table, precision=precise),
     )
-    real_wide = lax.all_to_all(real_part, "grid", split_axis=2, concat_axis=1, tiled=True)
+    real_wide = jnp.concatenate(
+        lax.all_to_all(
+            jnp.stack(jnp.split(real_part, lax.axis_size("grid"), axis=2)), "grid", 0, 0
+        ),
+        axis=1,
+    )
     imag_wide = lax.all_to_all(imag_part, "grid", split_axis=2, concat_axis=1, tiled=True)
     ahead_real = (
         jnp.einsum("pxyz,xk->pkyz", real_wide, cos_table, precision=precise)

time: 417 us -> 418 us (level)
  waiting for transfers between devices: 220 us -> 213 us
  local copies, waits for them, and re-layouts: 23.3 us -> 29.4 us
    unnamed x18 -> x30, local copies, waits for them, and re-layouts: 1.98 us -> 10.2 us
    all_to_all x2, waiting for transfers between devices: 34.3 us -> 28.3 us  [filtered(): lax.all_to_all(jnp.stack(jnp.split(real_part, lax.axis_size('grid'), axis...]
    all_to_all x2, waiting for transfers between devices: 33.2 us -> 28.1 us  [filtered(): lax.all_to_all(back_imag, 'grid', split_axis=1, concat_axis=2, tiled=True)]
  transfers between devices with their start and end apart: 10 -> 10, of which waited for: 10 -> 10; matrix products, arithmetic and copies ran while one was open for 16% -> 17% of each run, Pallas kernels for 0% -> 0%
where the time goes in v1:
time: 418 us; the launch traced here: 412 us
  waiting for transfers between devices  213 us (51%)
  matrix products  74.8 us (18%)
  starting transfers between devices  34.6 us (8%)
  local copies, waits for them, and re-layouts  29.4 us (7%)
  blocking collectives  28.1 us (7%)
  other arithmetic  16.4 us (4%)
  between operations  14.9 us (4%)
    reduce_scatter x1, waiting for transfers between devices, local(): lax.psum_scatter(jnp.einsum('bk,bxyz->kxyz', own_weights, orbitals, preci...  41.9 us
    all_to_all x2, waiting for transfers between devices, filtered(): lax.all_to_all(imag_part, 'grid', split_axis=2, concat_axis=1, tiled=True)  41.6 us
    all_to_all x2, waiting for transfers between devices, filtered(): lax.all_to_all(back_real, 'grid', split_axis=1, concat_axis=2, tiled=True)  37.9 us
    all_gather x1, waiting for transfers between devices, local(): lax.all_gather(localized, 'band', axis=0, tiled=True)  35.5 us
    all_to_all x2, waiting for transfers between devices, filtered(): lax.all_to_all(jnp.stack(jnp.split(real_part, lax.axis_size('grid'), axis...  28.3 us
    all_to_all x2, waiting for transfers between devices, filtered(): lax.all_to_all(back_imag, 'grid', split_axis=1, concat_axis=2, tiled=True)  28.1 us
    psum x1, blocking collectives, local(): own_rows = lax.psum(partial_pick, 'grid')  23.1 us
    unnamed x30, local copies, waits for them, and re-layouts  10.2 us
  transfers between devices with their start and end apart: 10, of which 10 were waited for; matrix products, arithmetic and copies ran while one was open for 17% of the time, Pallas kernels for 0%

profile of v1, /device:TPU:0, one launch (start us, length us, event | category | flops | bytes accessed | tf_op | source)
XLA Modules:
  0.0 411.6 jit_solution(15783216000196142425)
XLA Ops:
  10.0 23.1 %psum.7 = f32[1,4]{1,0:T(1,128)S(1)} all-reduce(f32[1,4]{1,0:T(1,128)S(1)} %fusion.230), channel_id=1, replica_groups=mesh['band'=4,'grid'=8] {'grid'}, use_global_device_ids=true, to_apply=%region_0.1 | all-reduce | flops 4 | bytes 32 | tf_op jit(solution)/shard_map/psum | solution.py:130
  33.1 5.0 %all-gather = f32[4,1,4]{2,1,0:T(1,128)S(1)} all-gather(f32[1,1,4]{2,1,0:T(1,128)S(1)} %bitcast.389), channel_id=1, replica_groups=mesh['band'=4,'grid'=8] {'band'}, dimensions={0}, use_global_device_ids=true | all-gather | bytes 80 | tf_op jit(solution)/shard_map/all_gather | solution.py:131
  40.6 3.8 broadcast_multiply_fusion
  44.4 41.9 %reduce-scatter.2.cloned.1.call-done = f32[1,16,128,128]{3,2,1,0:T(8,128)} async-done(((f32[4,16,128,128]{3,2,1,0:T(8,128)}), f32[1,16,128,128]{3,2,1,0:T(8,128)}) %reduce-scatter.2.cloned.1.call-update) | async-done | bytes 1048592 | tf_op jit(solution)/shard_map/reduce_scatter | solution.py:136
  87.5 35.5 %all-gather.3.cloned.1.call-done = f32[4,16,128,128]{3,2,1,0:T(8,128)} async-done(((f32[1,16,128,128]{3,2,1,0:T(8,128)}), f32[4,16,128,128]{3,2,1,0:T(8,128)}) %all-gather.3.cloned.1.call-update) | async-done | bytes 4194320 | tf_op jit(solution)/shard_map/all_gather | solution.py:156
  123.0 8.5 %fusion = f32[4,16,128,128]{3,0,2,1:T(4,128)S(1)} fusion(f32[4,16,128,128]{3,2,1,0:T(8,128)} %all-gather.3.cloned.1.call-done, s32[4]{0:T(128)S(1)} %broadcast_select_fusion), kind=kOutput, calls=%fused_computation.1 | convolution fusion | flops 50331664 | bytes 8388624 | tf_op jit(solution)/shard_map/qm,mxyz->qxyz/dot_general | solution.py:114
  131.6 3.6 slice_multiply_fusion.3
  145.3 1.6 copy.190
  146.8 5.8 %all-to-all-start.5 = ((f32[1,16,128,128]{3,1,0,2:T(8,128)}), f32[1,16,128,128]{3,1,0,2:T(8,128)}, u32[]{:S(2)}, u32[]{:S(2)}) async-start(f32[1,16,128,128]{3,1,0,2:T(8,128)} %copy.190), calls=%async_computation.6 | async-start | bytes 2097152 | tf_op jit(solution)/shard_map/all_to_all | solution.py:65
  157.9 20.9 %all-to-all-done.5 = f32[1,16,128,128]{3,1,0,2:T(8,128)} async-done(((f32[1,16,128,128]{3,1,0,2:T(8,128)}), f32[1,16,128,128]{3,1,0,2:T(8,128)}, u32[]{:S(2)}, u32[]{:S(2)}) %all-to-all-start.5) | async-done | bytes 1048608 | tf_op jit(solution)/shard_map/all_to_all | solution.py:65
  178.8 3.6 all-to-all-start.4
  190.0 1.6 copy.164
  194.2 14.2 %all-to-all-done.4 = f32[8,1,16,16,128]{4,3,2,1,0:T(8,128)S(1)} async-done(((f32[8,1,16,16,128]{4,3,2,1,0:T(8,128)}), f32[8,1,16,16,128]{4,3,2,1,0:T(8,128)S(1)}, u32[]{:S(2)}, u32[]{:S(2)}) %all-to-all-start.4) | async-done | bytes 1048608 | tf_op jit(solution)/shard_map/all_to_all | solution.py:60
  209.4 3.6 all-to-all-start.1
  218.3 20.7 %all-to-all-done.1 = f32[1,16,128,128]{3,1,0,2:T(8,128)S(1)} async-done(((f32[1,16,128,128]{3,1,0,2:T(8,128)}), f32[1,16,128,128]{3,1,0,2:T(8,128)S(1)}, u32[]{:S(2)}, u32[]{:S(2)}) %all-to-all-start.1) | async-done | bytes 1048608 | tf_op jit(solution)/shard_map/all_to_all | solution.py:65
  239.0 4.6 %all-to-all-start = ((f32[8,1,16,16,128]{4,3,2,1,0:T(8,128)}), f32[8,1,16,16,128]{4,3,2,1,0:T(8,128)}, u32[]{:S(2)}, u32[]{:S(2)}) async-start(f32[8,1,16,16,128]{4,3,2,1,0:T(8,128)} %fusion.35), calls=%async_computation.1 | async-start | bytes 2097152 | tf_op jit(solution)/shard_map/all_to_all | solution.py:60
  250.7 1.7 fusion.6
  253.6 1.6 copy.198
  255.2 14.1 %all-to-all-done = f32[8,1,16,16,128]{4,3,2,1,0:T(8,128)} async-done(((f32[8,1,16,16,128]{4,3,2,1,0:T(8,128)}), f32[8,1,16,16,128]{4,3,2,1,0:T(8,128)}, u32[]{:S(2)}, u32[]{:S(2)}) %all-to-all-start) | async-done | bytes 1048608 | tf_op jit(solution)/shard_map/all_to_all | solution.py:60
  269.3 4.4 %all-to-all-start.6 = ((f32[1,128,16,128]{3,2,0,1:T(8,128)}), f32[1,128,16,128]{3,2,0,1:T(8,128)}, u32[]{:S(2)}, u32[]{:S(2)}) async-start(f32[1,128,16,128]{3,2,0,1:T(8,128)} %copy.198), calls=%async_computation.7 | async-start | bytes 2097152 | tf_op jit(solution)/shard_map/all_to_all | solution.py:80
  277.9 21.3 %all-to-all-done.6 = f32[1,128,16,128]{3,2,0,1:T(8,128)} async-done(((f32[1,128,16,128]{3,2,0,1:T(8,128)}), f32[1,128,16,128]{3,2,0,1:T(8,128)}, u32[]{:S(2)}, u32[]{:S(2)}) %all-to-all-start.6) | async-done | bytes 1048608 | tf_op jit(solution)/shard_map/all_to_all | solution.py:80
  299.1 4.2 %all-to-all-start.7 = ((f32[1,128,16,128]{3,2,0,1:T(8,128)}), f32[1,128,16,128]{3,2,0,1:T(8,128)}, u32[]{:S(2)}, u32[]{:S(2)}) async-start(f32[1,128,16,128]{3,2,0,1:T(8,128)} %copy.203), calls=%async_computation.8 | async-start | bytes 2097152 | tf_op jit(solution)/shard_map/all_to_all | solution.py:81
  304.8 2.7 fusion.25
  310.3 2.9 fusion.14
  314.5 1.6 copy.172
  316.1 12.7 %all-to-all-done.7 = f32[1,128,16,128]{3,2,0,1:T(8,128)} async-done(((f32[1,128,16,128]{3,2,0,1:T(8,128)}), f32[1,128,16,128]{3,2,0,1:T(8,128)}, u32[]{:S(2)}, u32[]{:S(2)}) %all-to-all-start.7) | async-done | bytes 1048608 | tf_op jit(solution)/shard_map/all_to_all | solution.py:81
  328.8 4.0 all-to-all-start.2
  339.6 2.3 fusion.70
  341.9 16.6 %all-to-all-done.2 = f32[1,128,16,128]{3,2,0,1:T(8,128)S(1)} async-done(((f32[1,128,16,128]{3,2,0,1:T(8,128)}), f32[1,128,16,128]{3,2,0,1:T(8,128)S(1)}, u32[]{:S(2)}, u32[]{:S(2)}) %all-to-all-start.2) | async-done | bytes 1048608 | tf_op jit(solution)/shard_map/all_to_all | solution.py:80
  358.5 4.2 %all-to-all-start.3 = ((f32[1,128,16,128]{3,2,0,1:T(8,128)}), f32[1,128,16,128]{3,2,0,1:T(8,128)}, u32[]{:S(2)}, u32[]{:S(2)}) async-start(f32[1,128,16,128]{3,2,0,1:T(8,128)} %copy.177), calls=%async_computation.4 | async-start | bytes 2097152 | tf_op jit(solution)/shard_map/all_to_all | solution.py:81
  373.0 15.4 %all-to-all-done.3 = f32[1,128,16,128]{3,2,0,1:T(8,128)} async-done(((f32[1,128,16,128]{3,2,0,1:T(8,128)}), f32[1,128,16,128]{3,2,0,1:T(8,128)}, u32[]{:S(2)}, u32[]{:S(2)}) %all-to-all-start.3) | async-done | bytes 1048608 | tf_op jit(solution)/shard_map/all_to_all | solution.py:81
  400.0 4.5 %multiply_add_fusion = f32[1,16,128,128]{3,0,2,1:T(1,128)} fusion(f32[1,16,128,128]{3,0,2,1:T(1,128)S(1)} %bitcast.372, f32[1,16,128,128]{3,0,2,1:T(1,128)S(1)} %bitcast.371, f32[1,16,128,128]{3,0,2,1:T(1,128)S(1)} %bitcast.374, f32[1,16,128,128]{3,0,2,1:T(1,128)S(1)} %bitcast.373, f32[4,16,128,128]{3,0,2,1:T(4,128)S(1)} %copy-done.1), kind=kLoop, calls=%fused_computation.49 | loop fusion | flops 1835008 | bytes 9437184 | tf_op jit(solution)/shard_map/add | solution.py:164
  (111 shorter events, 84.4 us)
Async XLA Ops:
  7.2 79.2 %reduce-scatter.2.cloned.1.call-start = ((), (), s32[]{:S(2)}) async-start(), calls=%async_computation.9 | async-start | bytes 5242880 | tf_op jit(solution)/shard_map/reduce_scatter | solution.py:136
  44.4 78.6 %all-gather.3.cloned.1.call-start = ((), (), s32[]{:S(2)}) async-start(), calls=%async_computation.10 | async-start | bytes 5242880 | tf_op jit(solution)/shard_map/all_gather | solution.py:156
  87.5 44.1 %copy-start.2 = (f32[1,16,128,128]{3,2,1,0:T(8,128)S(1)}, f32[1,16,128,128]{3,2,1,0:T(8,128)}, u32[]{:S(2)}) copy-start(f32[1,16,128,128]{3,2,1,0:T(8,128)} %reduce-scatter.2.cloned.1.call-done) | copy-start | bytes 3145732
  131.6 3.6 copy-start
  146.8 32.0 %all-to-all-start.5 = ((f32[1,16,128,128]{3,1,0,2:T(8,128)}), f32[1,16,128,128]{3,1,0,2:T(8,128)}, u32[]{:S(2)}, u32[]{:S(2)}) async-start(f32[1,16,128,128]{3,1,0,2:T(8,128)} %copy.190), calls=%async_computation.6 | async-start | bytes 2097152 | tf_op jit(solution)/shard_map/all_to_all | solution.py:65
  178.8 29.6 %all-to-all-start.4 = ((f32[8,1,16,16,128]{4,3,2,1,0:T(8,128)}), f32[8,1,16,16,128]{4,3,2,1,0:T(8,128)S(1)}, u32[]{:S(2)}, u32[]{:S(2)}) async-start(f32[8,1,16,16,128]{4,3,2,1,0:T(8,128)} %fusion.27), calls=%async_computation.5 | async-start | bytes 2097152 | tf_op jit(solution)/shard_map/all_to_all | solution.py:60
  208.4 1.0 copy-start.4
  209.4 29.6 %all-to-all-start.1 = ((f32[1,16,128,128]{3,1,0,2:T(8,128)}), f32[1,16,128,128]{3,1,0,2:T(8,128)S(1)}, u32[]{:S(2)}, u32[]{:S(2)}) async-start(f32[1,16,128,128]{3,1,0,2:T(8,128)} %copy.164), calls=%async_computation.2 | async-start | bytes 2097152 | tf_op jit(solution)/shard_map/all_to_all | solution.py:65
  213.0 33.3 %copy-start.5 = (f32[8,1,16,16,128]{4,3,2,1,0:T(8,128)S(1)}, f32[8,1,16,16,128]{4,3,2,1,0:T(8,128)}, u32[]{:S(2)}) copy-start(f32[8,1,16,16,128]{4,3,2,1,0:T(8,128)} %copy-done.4) | copy-start | bytes 3145732
  239.0 30.3 %all-to-all-start = ((f32[8,1,16,16,128]{4,3,2,1,0:T(8,128)}), f32[8,1,16,16,128]{4,3,2,1,0:T(8,128)}, u32[]{:S(2)}, u32[]{:S(2)}) async-start(f32[8,1,16,16,128]{4,3,2,1,0:T(8,128)} %fusion.35), calls=%async_computation.1 | async-start | bytes 2097152 | tf_op jit(solution)/shard_map/all_to_all | solution.py:60
  247.9 2.8 copy-start.6
  269.3 29.8 %all-to-all-start.6 = ((f32[1,128,16,128]{3,2,0,1:T(8,128)}), f32[1,128,16,128]{3,2,0,1:T(8,128)}, u32[]{:S(2)}, u32[]{:S(2)}) async-start(f32[1,128,16,128]{3,2,0,1:T(8,128)} %copy.198), calls=%async_computation.7 | async-start | bytes 2097152 | tf_op jit(solution)/shard_map/all_to_all | solution.py:80
  299.1 29.7 %all-to-all-start.7 = ((f32[1,128,16,128]{3,2,0,1:T(8,128)}), f32[1,128,16,128]{3,2,0,1:T(8,128)}, u32[]{:S(2)}, u32[]{:S(2)}) async-start(f32[1,128,16,128]{3,2,0,1:T(8,128)} %copy.203), calls=%async_computation.8 | async-start | bytes 2097152 | tf_op jit(solution)/shard_map/all_to_all | solution.py:81
  328.8 29.7 %all-to-all-start.2 = ((f32[1,128,16,128]{3,2,0,1:T(8,128)}), f32[1,128,16,128]{3,2,0,1:T(8,128)S(1)}, u32[]{:S(2)}, u32[]{:S(2)}) async-start(f32[1,128,16,128]{3,2,0,1:T(8,128)} %copy.172), calls=%async_computation.3 | async-start | bytes 2097152 | tf_op jit(solution)/shard_map/all_to_all | solution.py:80
  358.5 5.5 %copy-start.7 = (f32[1,128,16,128]{3,2,0,1:T(8,128)}, f32[1,128,16,128]{3,2,0,1:T(8,128)S(1)}, u32[]{:S(2)}) copy-start(f32[1,128,16,128]{3,2,0,1:T(8,128)S(1)} %all-to-all-done.2) | copy-start | bytes 3145732
  358.5 29.9 %all-to-all-start.3 = ((f32[1,128,16,128]{3,2,0,1:T(8,128)}), f32[1,128,16,128]{3,2,0,1:T(8,128)}, u32[]{:S(2)}, u32[]{:S(2)}) async-start(f32[1,128,16,128]{3,2,0,1:T(8,128)} %copy.177), calls=%async_computation.4 | async-start | bytes 2097152 | tf_op jit(solution)/shard_map/all_to_all | solution.py:81
  364.0 4.0 copy-start.3
  396.3 3.7 copy-start.1
Sparse Core Ops, SparseCore 0:
  44.5 41.7 reduce-scatter.1
  88.5 34.4 all-gather.2
